TPU v7x, 32 devices: a whole 2x2x4 slice. The times are simulated.
32 devices in a mesh: fsdp: 4 (over y, core), ctx: 2 (over x), tp: 4 (over z).
Axes of the slice: x: 2, y: 2, z: 4, core: 2. Of those that a mesh axis runs over, the one named last changes fastest.
Arguments:
- tokens: bfloat16 [4, 1024, 2048], P('fsdp', 'ctx'), may hold values from -6 to 6
- lengths: int32 [4, 3], P('fsdp'), may hold values from 1 to 768, 960 in all within a row
- block_order: int32 [4, 4], P('fsdp'), may hold values from 0 to 3, each once within a row
- ln_gain: bfloat16 [2048], P('fsdp'), may hold values from 0.25 to 1.75
- ln_bias: bfloat16 [2048], P('fsdp'), may hold values from -3 to 3
- qkv_weight: bfloat16 [2048, 3, 2048], P('fsdp', None, 'tp'), may hold values from -0.125 to 0.125
- qkv_bias: bfloat16 [3, 2048], P(None, 'tp'), may hold values from -0.59765625 to 0.59765625
- dense_weight: bfloat16 [2048, 2048], P('fsdp', 'tp'), may hold values from -1 to 1
- dense_bias: bfloat16 [2048], P('fsdp'), may hold values from -3 to 3
- fc1_weight: bfloat16 [2048, 8192], P('fsdp', 'tp'), may hold values from -0.125 to 0.125
- fc1_bias: bfloat16 [8192], P('tp'), may hold values from -3 to 3
- fc2_weight: bfloat16 [2048, 8192], P('fsdp', 'tp'), may hold values from -0.0625 to 0.0625
- fc2_bias: bfloat16 [2048], P('fsdp'), may hold values from -3 to 3
- cotangent: bfloat16 [4, 1024, 2048], P('fsdp', 'ctx'), may hold values from -6 to 6
Outputs:
- output: bfloat16 [4, 1024, 2048], P('fsdp', 'ctx')
- input_grad: float32 [4, 1024, 2048], P('fsdp', 'ctx')
- ln_gain_grad: float32 [2048], P('fsdp')
- ln_bias_grad: float32 [2048], P('fsdp')
- qkv_weight_grad: float32 [2048, 3, 2048], P('fsdp', None, 'tp')
- qkv_bias_grad: float32 [3, 2048], P(None, 'tp')
- dense_weight_grad: float32 [2048, 2048], P('fsdp', 'tp')
- dense_bias_grad: float32 [2048], P('fsdp')
- fc1_weight_grad: float32 [2048, 8192], P('fsdp', 'tp')
- fc1_bias_grad: float32 [8192], P('tp')
- fc2_weight_grad: float32 [2048, 8192], P('fsdp', 'tp')
- fc2_bias_grad: float32 [2048], P('fsdp')
Inputs may be any that keep to these rules, and one draw needn't show every extreme that they name: Each row holds the lengths of 3 sequences packed from the row's start; they sum to 960 and the largest is exactly 768. Each row is a permutation of the 4 block numbers; dealt block j holds packed block block_order[b, j].
All inputs are finite; a program needn't handle non-finite values.
Results may differ from a plain program's by a relative error of at most 0.012.
Values may be sent and summed in bfloat16 or wider, within the bound.
No kernel may reach another device: no remote copies, remote signals or barrier semaphores. Data moves between devices by JAX's collectives and lax.ppermute only.
A program may use at most 256 MiB of HBM per device.

v0:
```python
import math
import jax
import jax.numpy as jnp
from jax import lax
from jax.sharding import PartitionSpec as P

HD = 256
ROT = 64
NORM_EPSILON = 1e-05
MASK_FLOOR = -1000000000.0


def rotation_tables(position):
    frequency = jnp.exp(jnp.arange(ROT // 2, dtype=jnp.float32) * (-2.0 * math.log(10000.0) / ROT))
    angles = position.astype(jnp.float32)[:, None] * frequency[None, :]
    return (jnp.cos(angles)[:, None, :], jnp.sin(angles)[:, None, :])


def rotate(values, cosine_table, sine_table):
    first_half = values[..., : ROT // 2]
    second_half = values[..., ROT // 2 : ROT]
    return jnp.concatenate(
        [
            first_half * cosine_table - second_half * sine_table,
            second_half * cosine_table + first_half * sine_table,
            values[..., ROT:],
        ],
        axis=-1,
    )


def rotate_back(grads, cosine_table, sine_table):
    first_half = grads[..., : ROT // 2]
    second_half = grads[..., ROT // 2 : ROT]
    return jnp.concatenate(
        [
            first_half * cosine_table + second_half * sine_table,
            second_half * cosine_table - first_half * sine_table,
            grads[..., ROT:],
        ],
        axis=-1,
    )


def packed_rows(order_row, first_slot, row_count, block_rows):
    row_index = jnp.arange(row_count, dtype=jnp.int32)
    dealt_slot = first_slot + row_index // block_rows
    selector = dealt_slot[:, None] == jnp.arange(order_row.shape[0], dtype=jnp.int32)[None, :]
    source_block = jnp.sum(jnp.where(selector, order_row[None, :], 0), axis=1, dtype=jnp.int32)
    return source_block * block_rows + row_index % block_rows


def place_rows(packed_at, lengths_row):
    seq_ends = jnp.cumsum(lengths_row, dtype=jnp.int32)
    passed = packed_at[:, None] >= seq_ends[None, :]
    segment = jnp.sum(passed.astype(jnp.int32), axis=1, dtype=jnp.int32)
    before = jnp.sum(jnp.where(passed, lengths_row[None, :], 0), axis=1, dtype=jnp.int32)
    return (segment, packed_at - before)


def gelu_slope(value):
    normal_cdf = 0.5 * (1.0 + lax.erf(value * (1.0 / math.sqrt(2.0))))
    density = jnp.exp(-0.5 * value * value) * (1.0 / math.sqrt(2.0 * math.pi))
    return normal_cdf + value * density


def per_device(
    tokens,
    lengths,
    block_order,
    ln_gain,
    ln_bias,
    qkv_weight,
    qkv_bias,
    dense_weight,
    dense_bias,
    fc1_weight,
    fc1_bias,
    fc2_weight,
    fc2_bias,
    cotangent,
):
    gathered = (
        lax.all_gather(qkv_weight, "fsdp", axis=0, tiled=True),
        lax.all_gather(dense_weight, "fsdp", axis=0, tiled=True),
        lax.all_gather(fc1_weight, "fsdp", axis=0, tiled=True),
        lax.all_gather(fc2_weight, "fsdp", axis=0, tiled=True),
        lax.all_gather(ln_gain, "fsdp", axis=0, tiled=True),
        lax.all_gather(ln_bias, "fsdp", axis=0, tiled=True),
        lax.all_gather(dense_bias, "fsdp", axis=0, tiled=True),
        lax.all_gather(fc2_bias, "fsdp", axis=0, tiled=True),
    )
    qkv_full = gathered[0]
    dense_full = gathered[1]
    fc1_full = gathered[2]
    fc2_full = gathered[3]
    norm_gain = gathered[4].astype(jnp.float32)
    norm_bias = gathered[5].astype(jnp.float32)
    out_bias = gathered[6].astype(jnp.float32) + gathered[7].astype(jnp.float32)
    inputs = tokens[0].astype(jnp.float32)
    row_count = inputs.shape[0]
    block_rows = row_count // 2
    group_rows = row_count * lax.axis_size("ctx")
    lengths_row = lengths[0]
    order_row = block_order[0]
    seq_count = lengths_row.shape[0]
    local_packed = packed_rows(order_row, lax.axis_index("ctx") * 2, row_count, block_rows)
    key_packed = packed_rows(order_row, 0, group_rows, block_rows)
    local_segment, local_position = place_rows(local_packed, lengths_row)
    key_segment = place_rows(key_packed, lengths_row)[0]
    valid_rows = (local_segment < seq_count).astype(jnp.float32)
    allowed = (local_segment[:, None] == key_segment[None, :]) & (
        key_packed[None, :] <= local_packed[:, None]
    )
    cosine_table, sine_table = rotation_tables(local_position)
    score_scale = 1.0 / math.sqrt(HD)
    row_mean = jnp.mean(inputs, axis=1, keepdims=True)
    centred = inputs - row_mean
    variance = jnp.mean(centred * centred, axis=1, keepdims=True)
    inverse = lax.rsqrt(variance + NORM_EPSILON)
    standard = centred * inverse
    normed = (standard * norm_gain + norm_bias).astype(jnp.bfloat16)
    projected = jnp.einsum(
        "td,dce->tce", normed, qkv_full, preferred_element_type=jnp.float32
    ) + qkv_bias.astype(jnp.float32)
    heads_here = projected.shape[2] // HD
    shaped = projected.reshape(row_count, 3, heads_here, HD)
    queries = rotate(shaped[:, 0], cosine_table, sine_table).astype(jnp.bfloat16)
    keys_local = rotate(shaped[:, 1], cosine_table, sine_table).astype(jnp.bfloat16)
    values_local = shaped[:, 2].astype(jnp.bfloat16)
    keys_all, values_all = (
        lax.all_gather(keys_local, "ctx", axis=0, tiled=True),
        lax.all_gather(values_local, "ctx", axis=0, tiled=True),
    )

    def head_scores(head_index):
        scores = (
            jnp.einsum(
                "qe,ke->qk",
                queries[:, head_index],
                keys_all[:, head_index],
                preferred_element_type=jnp.float32,
            )
            * score_scale
        )
        return jnp.where(allowed, scores, MASK_FLOOR)

    head_outputs = []
    log_totals = []
    for head_index in range(heads_here):
        scores = head_scores(head_index)
        row_max = jnp.max(scores, axis=1, keepdims=True)
        exp_scores = jnp.exp(scores - row_max)
        row_total = jnp.sum(exp_scores, axis=1, keepdims=True)
        probabilities = (exp_scores / row_total).astype(jnp.bfloat16)
        head_outputs.append(
            jnp.dot(probabilities, values_all[:, head_index], preferred_element_type=jnp.float32)
        )
        log_totals.append(row_max + jnp.log(row_total))
    attended = (
        (jnp.stack(head_outputs, axis=1) * valid_rows[:, None, None])
        .astype(jnp.bfloat16)
        .reshape(row_count, heads_here * HD)
    )
    pre_act = jnp.dot(normed, fc1_full, preferred_element_type=jnp.float32) + fc1_bias.astype(
        jnp.float32
    )
    hidden = jax.nn.gelu(pre_act, approximate=False).astype(jnp.bfloat16)
    partial_out = jnp.einsum(
        "te,de->td", attended, dense_full, preferred_element_type=jnp.float32
    ) + jnp.einsum("tf,df->td", hidden, fc2_full, preferred_element_type=jnp.float32)
    summed = lax.psum(partial_out, "tp")
    output = (inputs + summed + out_bias).astype(jnp.bfloat16)
    upstream_low = cotangent[0]
    upstream = upstream_low.astype(jnp.float32)
    out_bias_grad = jnp.sum(upstream, axis=0)
    dense_grad = jnp.einsum("td,te->de", upstream_low, attended, preferred_element_type=jnp.float32)
    fc2_grad = jnp.einsum("td,tf->df", upstream_low, hidden, preferred_element_type=jnp.float32)
    attended_grad = (
        jnp.dot(upstream_low, dense_full, preferred_element_type=jnp.float32).astype(jnp.bfloat16)
        * valid_rows[:, None].astype(jnp.bfloat16)
    ).reshape(row_count, heads_here, HD)
    hidden_grad = jnp.dot(upstream_low, fc2_full, preferred_element_type=jnp.float32)
    pre_grad = (hidden_grad * gelu_slope(pre_act)).astype(jnp.bfloat16)
    fc1_bias_grad = jnp.sum(pre_grad.astype(jnp.float32), axis=0)
    fc1_grad = jnp.einsum("td,tf->df", normed, pre_grad, preferred_element_type=jnp.float32)
    normed_grad = jnp.einsum("tf,df->td", pre_grad, fc1_full, preferred_element_type=jnp.float32)
    query_pieces = []
    key_pieces = []
    value_pieces = []
    for head_index in range(heads_here):
        probs_full = jnp.exp(head_scores(head_index) - log_totals[head_index])
        probs_low = probs_full.astype(jnp.bfloat16)
        head_grad = attended_grad[:, head_index]
        prob_grad = jnp.einsum(
            "qe,ke->qk", head_grad, values_all[:, head_index], preferred_element_type=jnp.float32
        )
        row_delta = jnp.sum(probs_full * prob_grad, axis=1, keepdims=True)
        score_grad = (probs_full * (prob_grad - row_delta)).astype(jnp.bfloat16)
        query_pieces.append(
            jnp.dot(score_grad, keys_all[:, head_index], preferred_element_type=jnp.float32)
            * score_scale
        )
        key_pieces.append(
            jnp.einsum(
                "qk,qe->ke", score_grad, queries[:, head_index], preferred_element_type=jnp.float32
            )
            * score_scale
        )
        value_pieces.append(
            jnp.einsum("qk,qe->ke", probs_low, head_grad, preferred_element_type=jnp.float32)
        )
    own_keys, own_values = (
        lax.psum_scatter(jnp.stack(key_pieces, axis=1), "ctx", scatter_dimension=0, tiled=True),
        lax.psum_scatter(jnp.stack(value_pieces, axis=1), "ctx", scatter_dimension=0, tiled=True),
    )
    query_turned = rotate_back(jnp.stack(query_pieces, axis=1), cosine_table, sine_table)
    key_turned = rotate_back(own_keys, cosine_table, sine_table)
    proj_grad = (
        jnp.stack([query_turned, key_turned, own_values], axis=1)
        .astype(jnp.bfloat16)
        .reshape(row_count, 3, heads_here * HD)
    )
    qkv_bias_grad = jnp.sum(proj_grad.astype(jnp.float32), axis=0)
    qkv_grad = jnp.einsum("td,tce->dce", normed, proj_grad, preferred_element_type=jnp.float32)
    normed_grad = normed_grad + jnp.einsum(
        "tce,dce->td", proj_grad, qkv_full, preferred_element_type=jnp.float32
    )
    full_grad = lax.psum(normed_grad, "tp")
    gain_grad = jnp.sum(full_grad * standard, axis=0)
    shift_grad = jnp.sum(full_grad, axis=0)
    scaled = full_grad * norm_gain
    input_grad = upstream + inverse * (
        scaled
        - jnp.mean(scaled, axis=1, keepdims=True)
        - standard * jnp.mean(scaled * standard, axis=1, keepdims=True)
    )
    bias_sums = lax.psum((qkv_bias_grad, fc1_bias_grad), ("fsdp", "ctx"))
    reduced = (
        lax.psum_scatter(qkv_grad, ("fsdp", "ctx"), scatter_dimension=0, tiled=True),
        lax.psum_scatter(dense_grad, ("fsdp", "ctx"), scatter_dimension=0, tiled=True),
        lax.psum_scatter(fc1_grad, ("fsdp", "ctx"), scatter_dimension=0, tiled=True),
        lax.psum_scatter(fc2_grad, ("fsdp", "ctx"), scatter_dimension=0, tiled=True),
        lax.psum_scatter(gain_grad, ("fsdp", "ctx"), scatter_dimension=0, tiled=True),
        lax.psum_scatter(shift_grad, ("fsdp", "ctx"), scatter_dimension=0, tiled=True),
        lax.psum_scatter(out_bias_grad, ("fsdp", "ctx"), scatter_dimension=0, tiled=True),
    )
    shards = (
        lax.all_gather(reduced[0], "ctx", axis=0, tiled=True),
        lax.all_gather(reduced[1], "ctx", axis=0, tiled=True),
        lax.all_gather(reduced[2], "ctx", axis=0, tiled=True),
        lax.all_gather(reduced[3], "ctx", axis=0, tiled=True),
        lax.all_gather(reduced[4], "ctx", axis=0, tiled=True),
        lax.all_gather(reduced[5], "ctx", axis=0, tiled=True),
        lax.all_gather(reduced[6], "ctx", axis=0, tiled=True),
    )
    return (
        output[None],
        input_grad[None],
        shards[4],
        shards[5],
        shards[0],
        bias_sums[0],
        shards[1],
        shards[6],
        shards[2],
        bias_sums[1],
        shards[3],
        shards[6],
    )


def solution(mesh):
    placed = (
        P("fsdp", "ctx", None),
        P("fsdp", None),
        P("fsdp", None),
        P("fsdp"),
        P("fsdp"),
        P("fsdp", None, "tp"),
        P(None, "tp"),
        P("fsdp", "tp"),
        P("fsdp"),
        P("fsdp", "tp"),
        P("tp"),
        P("fsdp", "tp"),
        P("fsdp"),
        P("fsdp", "ctx", None),
    )
    return jax.shard_map(
        per_device,
        mesh=mesh,
        in_specs=placed,
        out_specs=(
            P("fsdp", "ctx", None),
            P("fsdp", "ctx", None),
            P("fsdp"),
            P("fsdp"),
            P("fsdp", None, "tp"),
            P(None, "tp"),
            P("fsdp", "tp"),
            P("fsdp"),
            P("fsdp", "tp"),
            P("tp"),
            P("fsdp", "tp"),
            P("fsdp"),
        ),
        check_vma=False,
    )
```

profile of v0, /device:TPU:0, one launch (start us, length us, event | category | flops | bytes accessed | tf_op | source)
XLA Modules:
  0.0 1210.0 jit_solution(16124537954326559841)
XLA Ops:
  7.3 2.7 copy.57
  11.0 6.2 all-gather.2
  17.2 5.5 all-gather.1
  24.5 34.9 %all-gather.19.cloned.1.call-done = bf16[2048,3,512]{0,2,1:T(8,128)(2,1)} async-done(((bf16[512,3,512]{0,2,1:T(8,128)(2,1)}), bf16[2048,3,512]{0,2,1:T(8,128)(2,1)}) %all-gather.19.cloned.1.call-update) | async-done | bytes 6291472 | tf_op jit(solution)/shard_map/all_gather | solution.py:84
  59.3 5.9 fusion.46
  65.6 1.0 subtract_convert_fusion.3
  69.2 14.3 %all-gather.23.cloned.1.call-done = bf16[2048,512]{1,0:T(8,128)(2,1)} async-done(((bf16[512,512]{1,0:T(8,128)(2,1)}), bf16[2048,512]{1,0:T(8,128)(2,1)}) %all-gather.23.cloned.1.call-update) | async-done | bytes 2097168 | tf_op jit(solution)/shard_map/all_gather | solution.py:85
  83.5 4.3 fusion.58
  87.8 2.1 slice.201
  90.0 0.9 pad_maximum_fusion.5
  90.9 16.0 %all-gather.21.cloned.1.call-done = bf16[1024,2,256]{0,2,1:T(8,128)(2,1)} async-done(((bf16[512,2,256]{0,2,1:T(8,128)(2,1)}), bf16[1024,2,256]{0,2,1:T(8,128)(2,1)}) %all-gather.21.cloned.1.call-update) | async-done | bytes 1048592 | tf_op jit(solution)/shard_map/all_gather | solution.py:132
  106.9 1.9 fusion.97
  109.4 1.6 fusion.98
  112.8 1.5 pad_maximum_fusion.1
  114.5 15.7 %all-gather.37.cloned.1.call-done = bf16[1024,1,2,256]{0,3,2,1:T(8,128)(2,1)} async-done(((bf16[512,1,2,256]{0,3,2,1:T(8,128)(2,1)}), bf16[1024,1,2,256]{0,3,2,1:T(8,128)(2,1)}) %all-gather.37.cloned.1.call-update) | async-done | bytes 1048592 | tf_op jit(solution)/shard_map/all_gather | solution.py:133
  130.2 2.5 multiply_reduce_fusion.2
  137.1 1.5 pad_maximum_fusion
  140.1 2.4 convolution_bitcast_fusion.4
  144.2 3.3 convolution_bitcast_fusion.1
  147.5 1.9 fusion.57
  149.4 2.0 fusion.56
  152.3 12.5 %reduce-scatter.9.cloned.1.call-done = f32[512,2,256]{2,0,1:T(8,128)} async-done(((f32[1024,2,256]{2,0,1:T(8,128)}), f32[512,2,256]{2,0,1:T(8,128)}) %reduce-scatter.9.cloned.1.call-update) | async-done | bytes 1048592 | tf_op jit(solution)/shard_map/reduce_scatter | solution.py:215
  164.9 2.1 convert.64
  166.9 2.0 copy.60
  169.0 2.1 copy.63
  171.0 28.4 %reduce-scatter.7.cloned.1.call-done = f32[512,2,256]{0,2,1:T(8,128)} async-done(((f32[1024,2,256]{0,2,1:T(8,128)}), f32[512,2,256]{0,2,1:T(8,128)}) %reduce-scatter.7.cloned.1.call-update) | async-done | bytes 1048592 | tf_op jit(solution)/shard_map/reduce_scatter | solution.py:214
  199.5 1.2 slice.202
  200.7 1.4 add_convert_fusion.1
  202.0 1.0 pad_maximum_fusion.7
  203.1 2.1 copy.61
  205.1 2.1 copy.62
  207.2 8.8 fusion.40
  216.7 42.6 %all-gather.25.cloned.1.call-done = bf16[2048,2048]{1,0:T(8,128)(2,1)} async-done(((bf16[512,2048]{1,0:T(8,128)(2,1)}), bf16[2048,2048]{1,0:T(8,128)(2,1)}) %all-gather.25.cloned.1.call-update) | async-done | bytes 8388624 | tf_op jit(solution)/shard_map/all_gather | solution.py:86
  259.3 17.2 %fusion.20 = (bf16[512,2048]{1,0:T(8,128)(2,1)}, f32[512,2048]{1,0:T(8,128)}) fusion(f32[2048]{0:T(1024)S(1)} %convert_element_type.135, bf16[2048,2048]{1,0:T(8,128)(2,1)} %all-gather.25.cloned.1.call-done, bf16[1,512,2048]{2,1,0:T(8,128)(2,1)S(1)} %copy-done, f32[2048]{0:T(1024)S(1)} %bitcast.223, f32[2048]{0:T(1024)S(1)} %bitcast.214, ...), kind=kOutput, calls=%fused_computation.27 | convolution fusion | flops 4370464768 | bytes 16805888 | tf_op jit(solution)/shard_map/dot_general | solution.py:165
  276.5 42.7 %all-gather.27.cloned.1.call-done = bf16[2048,2048]{1,0:T(8,128)(2,1)} async-done(((bf16[512,2048]{1,0:T(8,128)(2,1)}), bf16[2048,2048]{1,0:T(8,128)(2,1)}) %all-gather.27.cloned.1.call-update) | async-done | bytes 8388624 | tf_op jit(solution)/shard_map/all_gather | solution.py:87
  319.2 9.4 convert_reduce_fusion.2
  328.6 1.3 copy-done.41
  329.9 8.8 fusion.92
  339.2 12.5 %convolution_bitcast_fusion = f32[2048,2048]{0,1:T(8,128)} fusion(bf16[512,2048]{1,0:T(8,128)(2,1)} %get-tuple-element.96, bf16[1,512,2048]{2,1,0:T(8,128)(2,1)} %param.27), kind=kOutput, calls=%fused_computation | convolution fusion | flops 4294967296 | bytes 20971520 | tf_op jit(solution)/shard_map/td,tf->df/dot_general | solution.py:178
  352.4 0.9 fusion.63
  353.3 10.8 fusion.99
  364.1 9.8 fusion.100
  374.5 6.5 convolution_add_fusion
  381.0 8.7 bitcast_add_fusion
  389.8 79.9 %reduce-scatter.11.cloned.1.call-done = f32[256,3,512]{2,0,1:T(8,128)} async-done(((f32[2048,3,512]{2,0,1:T(8,128)}), f32[256,3,512]{2,0,1:T(8,128)}) %reduce-scatter.11.cloned.1.call-update) | async-done | bytes 1572880 | tf_op jit(solution)/shard_map/reduce_scatter | solution.py:240
  469.7 119.7 %reduce-scatter.15.cloned.1.call-done = f32[256,2048]{1,0:T(8,128)} async-done(((f32[2048,2048]{1,0:T(8,128)}), f32[256,2048]{1,0:T(8,128)}) %reduce-scatter.15.cloned.1.call-update) | async-done | bytes 2097168 | tf_op jit(solution)/shard_map/reduce_scatter | solution.py:242
  589.5 119.4 %reduce-scatter.17.cloned.1.call-done = f32[256,2048]{0,1:T(8,128)} async-done(((f32[2048,2048]{0,1:T(8,128)}), f32[256,2048]{0,1:T(8,128)}) %reduce-scatter.17.cloned.1.call-update) | async-done | bytes 2097168 | tf_op jit(solution)/shard_map/reduce_scatter | solution.py:243
  710.2 5.2 all-gather.4
  715.4 5.2 all-gather.3
  720.6 1.3 convert_reduce_fusion.3
  721.9 9.8 all-gather.31.cloned.1.call-done
  731.8 2.5 copy.66
  734.3 291.4 %all-reduce.7.cloned.1.call-done = (f32[512,2048]{1,0:T(8,128)}, f32[512,2048]{1,0:T(8,128)}) async-done(((f32[512,2048]{1,0:T(8,128)}, f32[512,2048]{1,0:T(8,128)}), (f32[512,2048]{1,0:T(8,128)}, f32[512,2048]{1,0:T(8,128)})) %all-reduce.7.cloned.1.call-update) | async-done | bytes 8388624 | tf_op jit(solution)/shard_map/psum | solution.py:172
  1025.7 3.9 fusion.13
  1029.8 6.1 convert_reduce_fusion
  1035.8 28.5 %all-reduce.3 = (f32[2048]{0:T(1024)S(1)}, f32[2048]{0:T(1024)S(1)}, f32[3,512]{1,0:T(4,128)}, f32[2048]{0:T(1024)S(1)}, f32[2048]{0:T(1024)}) all-reduce(f32[2048]{0:T(1024)S(1)} %get-tuple-element.60, f32[2048]{0:T(1024)S(1)} %get-tuple-element.63, ...), channel_id=5, replica_groups=mesh['fsdp'=4,'ctx'=2,'tp'=4] {'fsdp','ctx'}, use_global_device_ids=true, to_apply=%region_21.22.clone | all-reduce | flops 9728 | bytes 77824
  1064.4 4.4 all-gather.7
  1068.9 4.3 all-gather.5
  1073.2 4.2 all-gather.6
  1077.5 54.2 %all-gather.33.cloned.1.call-done = f32[512,2048]{1,0:T(8,128)} async-done(((f32[256,2048]{1,0:T(8,128)}), f32[512,2048]{1,0:T(8,128)}) %all-gather.33.cloned.1.call-update) | async-done | bytes 4194320 | tf_op jit(solution)/shard_map/all_gather | solution.py:251
  1131.6 58.1 %all-gather.35.cloned.1.call-done = f32[512,2048]{0,1:T(8,128)} async-done(((f32[256,2048]{0,1:T(8,128)}), f32[512,2048]{0,1:T(8,128)}) %all-gather.35.cloned.1.call-update) | async-done | bytes 4194320 | tf_op jit(solution)/shard_map/all_gather | solution.py:252
  1189.8 5.3 copy.67
  1196.9 3.9 copy.84
  1201.3 2.0 copy.86
  (175 shorter events, 22.4 us)
Async XLA Ops:
  7.2 3.7 copy-start.32
  7.2 3.8 copy-start.33
  7.2 3.8 copy-start.34
  7.2 15.5 %copy-start.30 = (bf16[3,512]{1,0:T(4,128)(2,1)S(1)}, bf16[3,512]{1,0:T(4,128)(2,1)}, u32[]{:S(2)}) copy-start(bf16[3,512]{1,0:T(4,128)(2,1)} %param.20) | copy-start | bytes 9220
  7.2 15.5 %copy-start.37 = (s32[1,3]{1,0:T(1,128)S(1)}, s32[1,3]{1,0:T(1,128)}, u32[]{:S(2)}) copy-start(s32[1,3]{1,0:T(1,128)} %param.15) | copy-start | bytes 40
  7.2 15.8 %copy-start = (bf16[1,512,2048]{2,1,0:T(8,128)(2,1)S(1)}, bf16[1,512,2048]{2,1,0:T(8,128)(2,1)}, u32[]{:S(2)}) copy-start(bf16[1,512,2048]{2,1,0:T(8,128)(2,1)} %param.14) | copy-start | bytes 6291460
  7.2 52.1 %all-gather.19.cloned.1.call-start = ((), (), s32[]{:S(2)}) async-start(), calls=%async_computation.6 | async-start | bytes 7864320 | tf_op jit(solution)/shard_map/all_gather | solution.py:84
  10.0 73.5 %all-gather.23.cloned.1.call-start = ((), (), s32[]{:S(2)}) async-start(), calls=%async_computation.8 | async-start | bytes 2621440 | tf_op jit(solution)/shard_map/all_gather | solution.py:85
  10.8 96.1 %all-gather.21.cloned.1.call-start = ((), (), s32[]{:S(2)}) async-start(), calls=%async_computation.7 | async-start | bytes 1572864 | tf_op jit(solution)/shard_map/all_gather | solution.py:132
  11.0 12.1 copy-start.26
  17.2 48.0 %copy-start.28 = (f32[4,1,512]{2,1,0:T(1,128)}, f32[4,1,512]{2,1,0:T(1,128)S(1)}, u32[]{:S(2)}) copy-start(f32[4,1,512]{2,1,0:T(1,128)S(1)} %convert_element_type.153) | copy-start | bytes 24580
  23.0 45.6 %copy-start.27 = (s32[512]{0:T(512)}, s32[512]{0:T(512)S(1)}, u32[]{:S(2)}) copy-start(s32[512]{0:T(512)S(1)} %get-tuple-element.65) | copy-start | bytes 6148
  24.5 41.1 %copy-start.21 = (f32[512,32]{0,1:T(8,128)}, f32[512,32]{0,1:T(8,128)S(1)}, u32[]{:S(2)}) copy-start(f32[512,32]{0,1:T(8,128)S(1)} %get-tuple-element.92) | copy-start | bytes 196612
  24.5 41.1 %copy-start.22 = (f32[512,32]{0,1:T(8,128)}, f32[512,32]{0,1:T(8,128)S(1)}, u32[]{:S(2)}) copy-start(f32[512,32]{0,1:T(8,128)S(1)} %get-tuple-element.93) | copy-start | bytes 196612
  65.3 1.7 copy-start.12
  67.8 62.4 %all-gather.37.cloned.1.call-start = ((), (), s32[]{:S(2)}) async-start(), calls=%async_computation.21 | async-start | bytes 1572864 | tf_op jit(solution)/shard_map/all_gather | solution.py:133
  68.0 19.8 %copy-start.25 = (s32[1024]{0:T(1024)}, s32[1024]{0:T(1024)S(1)}, u32[]{:S(2)}) copy-start(s32[1024]{0:T(1024)S(1)} %fusion.79) | copy-start | bytes 12292
  90.0 74.9 %reduce-scatter.9.cloned.1.call-start = ((), (), s32[]{:S(2)}) async-start(), calls=%async_computation.12 | async-start | bytes 3145728 | tf_op jit(solution)/shard_map/reduce_scatter | solution.py:215
  106.9 2.4 copy-start.38
  108.8 2.7 copy-start.1
  108.8 2.7 copy-start.13
  111.0 1.8 copy-start.3
  114.3 85.2 %reduce-scatter.7.cloned.1.call-start = ((), (), s32[]{:S(2)}) async-start(), calls=%async_computation.11 | async-start | bytes 3145728 | tf_op jit(solution)/shard_map/reduce_scatter | solution.py:214
  130.2 2.5 copy-start.4
  132.7 1.9 copy-start.2
  132.8 2.2 copy-start.19
  133.3 2.9 copy-start.10
  136.1 1.0 copy-start.11
  138.6 1.6 copy-start.20
  138.6 120.8 %all-gather.25.cloned.1.call-start = ((), (), s32[]{:S(2)}) async-start(), calls=%async_computation.9 | async-start | bytes 10485760 | tf_op jit(solution)/shard_map/all_gather | solution.py:86
  139.3 179.9 %all-gather.27.cloned.1.call-start = ((), (), s32[]{:S(2)}) async-start(), calls=%async_computation.10 | async-start | bytes 10485760 | tf_op jit(solution)/shard_map/all_gather | solution.py:87
  140.1 234.2 %reduce-scatter.13.cloned.1.call-start = ((), (), s32[]{:S(2)}) async-start(), calls=%async_computation.15 | async-start | bytes 4718592 | tf_op jit(solution)/shard_map/reduce_scatter | solution.py:241
  140.1 2.4 copy-start.5
  142.6 0.7 copy-start.23
  142.6 1.6 copy-start.7
  147.5 322.2 %reduce-scatter.11.cloned.1.call-start = ((), (), s32[]{:S(2)}) async-start(), calls=%async_computation.13 | async-start | bytes 14155776 | tf_op jit(solution)/shard_map/reduce_scatter | solution.py:240
  149.4 2.0 copy-start.17
  151.5 0.8 copy-start.18
  216.0 0.7 copy-start.31
  216.0 43.3 %copy-start.29 = (f32[4,1,512]{2,1,0:T(1,128)S(1)}, f32[4,1,512]{2,1,0:T(1,128)}, u32[]{:S(2)}) copy-start(f32[4,1,512]{2,1,0:T(1,128)} %copy-done.28) | copy-start | bytes 24580
  216.0 373.4 %reduce-scatter.15.cloned.1.call-start = ((), (), s32[]{:S(2)}) async-start(), calls=%async_computation.17 | async-start | bytes 18874368 | tf_op jit(solution)/shard_map/reduce_scatter | solution.py:242
  328.6 1.3 copy-start.41
  338.7 370.2 %reduce-scatter.17.cloned.1.call-start = ((), (), s32[]{:S(2)}) async-start(), calls=%async_computation.19 | async-start | bytes 18874368 | tf_op jit(solution)/shard_map/reduce_scatter | solution.py:243
  351.7 0.7 copy-start.24
  351.8 380.0 %all-gather.31.cloned.1.call-start = ((), (), s32[]{:S(2)}) async-start(), calls=%async_computation.16 | async-start | bytes 1572864 | tf_op jit(solution)/shard_map/all_gather | solution.py:250
  353.3 10.8 copy-start.42
  374.3 6.7 copy-start.14
  374.3 6.7 copy-start.15
  374.3 651.4 %all-reduce.7.cloned.1.call-start = ((), (), s32[]{:S(2)}) async-start(), calls=%async_computation.22 | async-start | bytes 16777216 | tf_op jit(solution)/shard_map/psum | solution.py:172
  374.5 6.5 copy-start.16
  374.5 6.5 copy-start.40
  389.7 319.2 %copy-start.35 = (bf16[512]{0:T(512)(128)(2,1)S(1)}, bf16[512]{0:T(512)(128)(2,1)}, u32[]{:S(2)}) copy-start(bf16[512]{0:T(512)(128)(2,1)} %param.22) | copy-start | bytes 3076
  389.8 319.2 %copy-start.36 = (bf16[512]{0:T(512)(128)(2,1)S(1)}, bf16[512]{0:T(512)(128)(2,1)}, u32[]{:S(2)}) copy-start(bf16[512]{0:T(512)(128)(2,1)} %param.26) | copy-start | bytes 3076
  389.8 319.2 %copy-start.39 = (u32[32]{0:T(128)S(1)}, u32[32]{0:T(128)}, u32[]{:S(2)}) copy-start(u32[32]{0:T(128)} %constant.160) | copy-start | bytes 388
  389.8 687.7 %all-gather.29.cloned.1.call-start = ((), (), s32[]{:S(2)}) async-start(), calls=%async_computation.14 | async-start | bytes 4718592 | tf_op jit(solution)/shard_map/all_gather | solution.py:249
  469.7 661.9 %all-gather.33.cloned.1.call-start = ((), (), s32[]{:S(2)}) async-start(), calls=%async_computation.18 | async-start | bytes 6291456 | tf_op jit(solution)/shard_map/all_gather | solution.py:251
  589.5 600.3 %all-gather.35.cloned.1.call-start = ((), (), s32[]{:S(2)}) async-start(), calls=%async_computation.20 | async-start | bytes 6291456 | tf_op jit(solution)/shard_map/all_gather | solution.py:252
  1025.7 3.9 copy-start.6
  1025.7 4.1 copy-start.8
  1195.1 6.2 copy-start.9
Sparse Core Ops, SparseCore 0:
  10.2 49.1 all-gather.18
  60.9 22.5 all-gather.22
  85.6 21.2 all-gather.20
  108.9 21.2 all-gather.36
  132.9 31.9 reduce-scatter.8
  167.5 31.8 reduce-scatter.6
  201.0 58.2 all-gather.24
  260.9 58.2 all-gather.26
  323.1 51.0 reduce-scatter.12
  377.6 92.0 reduce-scatter.10
  473.2 116.1 reduce-scatter.14
  592.9 115.9 reduce-scatter.16
  710.4 21.2 all-gather.30
  734.8 290.8 all-reduce.6
  1027.0 46.3 all-gather.28
  1074.9 56.7 all-gather.32
  1133.0 56.7 all-gather.34
where the time goes:
time: 1220 us; the launch traced here: 1210 us
  waiting for transfers between devices  942 us (77%)
  matrix products  122 us (10%)
  blocking collectives  63.4 us (5%)
  local copies, waits for them, and re-layouts  37.8 us (3%)
  other arithmetic  27.6 us (2%)
  between operations  15.6 us (1%)
    psum x1, waiting for transfers between devices, per_device(): summed = lax.psum(partial_out, 'tp')  291 us
    reduce_scatter x1, waiting for transfers between devices, per_device(): lax.psum_scatter(fc1_grad, ('fsdp', 'ctx'), scatter_dimension=0, tiled=True)  120 us
    reduce_scatter x1, waiting for transfers between devices, per_device(): lax.psum_scatter(fc2_grad, ('fsdp', 'ctx'), scatter_dimension=0, tiled=True)  119 us
    reduce_scatter x1, waiting for transfers between devices, per_device(): lax.psum_scatter(qkv_grad, ('fsdp', 'ctx'), scatter_dimension=0, tiled=True)  79.9 us
    all_gather x1, waiting for transfers between devices, per_device(): lax.all_gather(reduced[3], 'ctx', axis=0, tiled=True)  58.1 us
    all_gather x1, waiting for transfers between devices, per_device(): lax.all_gather(reduced[2], 'ctx', axis=0, tiled=True)  54.2 us
    all_gather x1, waiting for transfers between devices, per_device(): lax.all_gather(fc2_weight, 'fsdp', axis=0, tiled=True)  42.7 us
    all_gather x1, waiting for transfers between devices, per_device(): lax.all_gather(fc1_weight, 'fsdp', axis=0, tiled=True)  42.6 us
  transfers between devices with their start and end apart: 17, of which 16 were waited for; matrix products, arithmetic and copies ran while one was open for 14% of the time, Pallas kernels for 0%

commit v1 on v0

--- a/solution.py
+++ b/solution.py
@@ -169,7 +169,7 @@
     partial_out = jnp.einsum(
         "te,de->td", attended, dense_full, preferred_element_type=jnp.float32
     ) + jnp.einsum("tf,df->td", hidden, fc2_full, preferred_element_type=jnp.float32)
-    summed = lax.psum(partial_out, "tp")
+    summed = jnp.sum(jax.lax.all_gather(partial_out, "tp"), axis=0)
     output = (inputs + summed + out_bias).astype(jnp.bfloat16)
     upstream_low = cotangent[0]
     upstream = upstream_low.astype(jnp.float32)

time: 1220 us -> 1370 us (1.12)
  waiting for transfers between devices: 942 us -> 1090 us
    all_gather x0 -> x1, waiting for transfers between devices: none -> 287 us  [per_device(): summed = jnp.sum(jax.lax.all_gather(partial_out, 'tp'), axis=0)]
    psum x1, waiting for transfers between devices: 291 us -> 155 us  [per_device(): full_grad = lax.psum(normed_grad, 'tp')]
    reduce_scatter x1, waiting for transfers between devices: 0.33 us -> 22.4 us  [per_device(): lax.psum_scatter(dense_grad, ('fsdp', 'ctx'), scatter_dimension=0, tiled=...]
  transfers between devices with their start and end apart: 17 -> 18, of which waited for: 16 -> 17; matrix products, arithmetic and copies ran while one was open for 14% -> 12% of each run, Pallas kernels for 0% -> 0%
where the time goes in v1:
time: 1370 us; the launch traced here: 1360 us
  waiting for transfers between devices  1090 us (80%)
  matrix products  114 us (8%)
  blocking collectives  63.7 us (5%)
  other arithmetic  38.9 us (3%)
  local copies, waits for them, and re-layouts  37.2 us (3%)
  between operations  16 us (1%)
    all_gather x1, waiting for transfers between devices, per_device(): summed = jnp.sum(jax.lax.all_gather(partial_out, 'tp'), axis=0)  287 us
    psum x1, waiting for transfers between devices, per_device(): full_grad = lax.psum(normed_grad, 'tp')  155 us
    reduce_scatter x1, waiting for transfers between devices, per_device(): lax.psum_scatter(fc2_grad, ('fsdp', 'ctx'), scatter_dimension=0, tiled=True)  119 us
    reduce_scatter x1, waiting for transfers between devices, per_device(): lax.psum_scatter(fc1_grad, ('fsdp', 'ctx'), scatter_dimension=0, tiled=True)  108 us
    reduce_scatter x1, waiting for transfers between devices, per_device(): lax.psum_scatter(qkv_grad, ('fsdp', 'ctx'), scatter_dimension=0, tiled=True)  78.6 us
    all_gather x1, waiting for transfers between devices, per_device(): lax.all_gather(reduced[3], 'ctx', axis=0, tiled=True)  58.2 us
    all_gather x1, waiting for transfers between devices, per_device(): lax.all_gather(fc2_weight, 'fsdp', axis=0, tiled=True)  42.6 us
    all_gather x1, waiting for transfers between devices, per_device(): lax.all_gather(fc1_weight, 'fsdp', axis=0, tiled=True)  42.6 us
  transfers between devices with their start and end apart: 18, of which 17 were waited for; matrix products, arithmetic and copies ran while one was open for 12% of the time, Pallas kernels for 0%

profile of v1, /device:TPU:0, one launch (start us, length us, event | category | flops | bytes accessed | tf_op | source)
XLA Modules:
  0.0 1361.0 jit_solution(3118643967423950156)
XLA Ops:
  7.3 2.7 copy.57
  11.0 6.2 all-gather.3
  17.2 5.5 all-gather.2
  24.5 34.9 %all-gather.21.cloned.1.call-done = bf16[2048,3,512]{0,2,1:T(8,128)(2,1)} async-done(((bf16[512,3,512]{0,2,1:T(8,128)(2,1)}), bf16[2048,3,512]{0,2,1:T(8,128)(2,1)}) %all-gather.21.cloned.1.call-update) | async-done | bytes 6291472 | tf_op jit(solution)/shard_map/all_gather | solution.py:84
  59.3 5.9 fusion.44
  68.7 14.8 %all-gather.25.cloned.1.call-done = bf16[2048,512]{1,0:T(8,128)(2,1)} async-done(((bf16[512,512]{1,0:T(8,128)(2,1)}), bf16[2048,512]{1,0:T(8,128)(2,1)}) %all-gather.25.cloned.1.call-update) | async-done | bytes 2097168 | tf_op jit(solution)/shard_map/all_gather | solution.py:85
  83.5 4.3 fusion.56
  87.8 2.1 slice.201
  90.9 16.0 %all-gather.23.cloned.1.call-done = bf16[1024,2,256]{0,2,1:T(8,128)(2,1)} async-done(((bf16[512,2,256]{0,2,1:T(8,128)(2,1)}), bf16[1024,2,256]{0,2,1:T(8,128)(2,1)}) %all-gather.23.cloned.1.call-update) | async-done | bytes 1048592 | tf_op jit(solution)/shard_map/all_gather | solution.py:132
  106.9 1.9 fusion.95
  109.4 1.6 fusion.96
  112.8 1.5 pad_maximum_fusion.1
  114.5 15.7 %all-gather.39.cloned.1.call-done = bf16[1024,1,2,256]{0,3,2,1:T(8,128)(2,1)} async-done(((bf16[512,1,2,256]{0,3,2,1:T(8,128)(2,1)}), bf16[1024,1,2,256]{0,3,2,1:T(8,128)(2,1)}) %all-gather.39.cloned.1.call-update) | async-done | bytes 1048592 | tf_op jit(solution)/shard_map/all_gather | solution.py:133
  130.2 2.5 multiply_reduce_fusion.2
  137.1 1.5 pad_maximum_fusion
  140.2 2.4 convolution_bitcast_fusion.4
  144.1 3.3 convolution_bitcast_fusion.1
  147.5 1.9 fusion.55
  149.4 2.0 fusion.54
  152.3 12.6 reduce-scatter.9.cloned.1.call-done
  164.9 2.1 convert.64
  166.9 2.0 copy.60
  169.0 2.0 copy.63
  171.0 28.5 %reduce-scatter.7.cloned.1.call-done = f32[512,2,256]{0,2,1:T(8,128)} async-done(((f32[1024,2,256]{0,2,1:T(8,128)}), f32[512,2,256]{0,2,1:T(8,128)}) %reduce-scatter.7.cloned.1.call-update) | async-done | bytes 1048592 | tf_op jit(solution)/shard_map/reduce_scatter | solution.py:214
  199.5 1.2 slice.202
  200.7 1.4 add_convert_fusion.1
  203.1 2.1 copy.61
  205.1 2.0 copy.62
  207.2 8.9 fusion.38
  216.7 42.6 %all-gather.27.cloned.1.call-done = bf16[2048,2048]{1,0:T(8,128)(2,1)} async-done(((bf16[512,2048]{1,0:T(8,128)(2,1)}), bf16[2048,2048]{1,0:T(8,128)(2,1)}) %all-gather.27.cloned.1.call-update) | async-done | bytes 8388624 | tf_op jit(solution)/shard_map/all_gather | solution.py:86
  259.3 17.2 %fusion.19 = (bf16[512,2048]{1,0:T(8,128)(2,1)}, f32[512,2048]{1,0:T(8,128)}) fusion(f32[2048]{0:T(1024)S(1)} %convert_element_type.137, bf16[2048,2048]{1,0:T(8,128)(2,1)} %all-gather.27.cloned.1.call-done, bf16[1,512,2048]{2,1,0:T(8,128)(2,1)S(1)} %copy-done, f32[2048]{0:T(1024)S(1)} %bitcast.215, f32[2048]{0:T(1024)S(1)} %bitcast.206, ...), kind=kOutput, calls=%fused_computation.27 | convolution fusion | flops 4370464768 | bytes 16805888 | tf_op jit(solution)/shard_map/dot_general | solution.py:165
  276.5 42.6 %all-gather.29.cloned.1.call-done = bf16[2048,2048]{1,0:T(8,128)(2,1)} async-done(((bf16[512,2048]{1,0:T(8,128)(2,1)}), bf16[2048,2048]{1,0:T(8,128)(2,1)}) %all-gather.29.cloned.1.call-update) | async-done | bytes 8388624 | tf_op jit(solution)/shard_map/all_gather | solution.py:87
  319.2 9.4 convert_reduce_fusion.2
  328.6 1.3 copy-done.43
  329.9 8.8 fusion.90
  339.2 12.5 convolution_bitcast_fusion
  351.8 22.4 %reduce-scatter.13.cloned.1.call-done = f32[256,512]{0,1:T(8,128)} async-done(((f32[2048,512]{0,1:T(8,128)}), f32[256,512]{0,1:T(8,128)}) %reduce-scatter.13.cloned.1.call-update) | async-done | bytes 524304 | tf_op jit(solution)/shard_map/reduce_scatter | solution.py:241
  374.3 7.7 fusion.98
  382.1 8.8 bitcast_add_fusion
  391.0 78.6 %reduce-scatter.11.cloned.1.call-done = f32[256,3,512]{2,0,1:T(8,128)} async-done(((f32[2048,3,512]{2,0,1:T(8,128)}), f32[256,3,512]{2,0,1:T(8,128)}) %reduce-scatter.11.cloned.1.call-update) | async-done | bytes 1572880 | tf_op jit(solution)/shard_map/reduce_scatter | solution.py:240
  469.9 7.8 fusion.97
  477.6 3.3 convolution_add_fusion
  481.1 108.4 %reduce-scatter.15.cloned.1.call-done = f32[256,2048]{1,0:T(8,128)} async-done(((f32[2048,2048]{1,0:T(8,128)}), f32[256,2048]{1,0:T(8,128)}) %reduce-scatter.15.cloned.1.call-update) | async-done | bytes 2097168 | tf_op jit(solution)/shard_map/reduce_scatter | solution.py:242
  589.5 119.4 %reduce-scatter.17.cloned.1.call-done = f32[256,2048]{0,1:T(8,128)} async-done(((f32[2048,2048]{0,1:T(8,128)}), f32[256,2048]{0,1:T(8,128)}) %reduce-scatter.17.cloned.1.call-update) | async-done | bytes 2097168 | tf_op jit(solution)/shard_map/reduce_scatter | solution.py:243
  710.2 5.2 all-gather.5
  715.4 5.3 all-gather.4
  720.8 1.3 convert_reduce_fusion.3
  722.1 9.7 all-gather.33.cloned.1.call-done
  731.7 2.5 copy.66
  734.3 155.3 %all-reduce.6.cloned.1.call-done = f32[512,2048]{1,0:T(8,128)} async-done(((f32[512,2048]{1,0:T(8,128)}), f32[512,2048]{1,0:T(8,128)}) %all-reduce.6.cloned.1.call-update) | async-done | bytes 4194320 | tf_op jit(solution)/shard_map/psum | solution.py:229
  889.5 3.8 fusion.13
  893.7 3.7 convert_reduce_fusion.1
  897.3 28.5 %all-reduce.3 = (f32[2048]{0:T(1024)S(1)}, f32[2048]{0:T(1024)S(1)}, f32[3,512]{1,0:T(4,128)}, f32[2048]{0:T(1024)S(1)}, f32[2048]{0:T(1024)}) all-reduce(f32[2048]{0:T(1024)S(1)} %get-tuple-element.60, f32[2048]{0:T(1024)S(1)} %get-tuple-element.63, ...), channel_id=6, replica_groups=mesh['fsdp'=4,'ctx'=2,'tp'=4] {'fsdp','ctx'}, use_global_device_ids=true, to_apply=%region_21.22.clone | all-reduce | flops 9728 | bytes 77824
  925.9 4.4 all-gather.8
  930.3 4.4 all-gather.6
  934.8 4.2 all-gather.7
  939.0 286.9 %all-gather.41.cloned.1.call-done = f32[2048,2048]{1,0:T(8,128)} async-done(((f32[512,2048]{1,0:T(8,128)}), f32[2048,2048]{1,0:T(8,128)}) %all-gather.41.cloned.1.call-update) | async-done | bytes 16777232 | tf_op jit(solution)/shard_map/all_gather | solution.py:172
  1226.0 10.5 reduce_sum.182
  1236.4 4.7 fusion.16
  1241.1 41.2 %all-gather.35.cloned.1.call-done = f32[512,2048]{1,0:T(8,128)} async-done(((f32[256,2048]{1,0:T(8,128)}), f32[512,2048]{1,0:T(8,128)}) %all-gather.35.cloned.1.call-update) | async-done | bytes 4194320 | tf_op jit(solution)/shard_map/all_gather | solution.py:251
  1282.3 58.2 %all-gather.37.cloned.1.call-done = f32[512,2048]{0,1:T(8,128)} async-done(((f32[256,2048]{0,1:T(8,128)}), f32[512,2048]{0,1:T(8,128)}) %all-gather.37.cloned.1.call-update) | async-done | bytes 4194320 | tf_op jit(solution)/shard_map/all_gather | solution.py:252
  1340.5 5.3 copy.67
  1347.5 3.9 copy.83
  1352.0 2.0 copy.85
  (182 shorter events, 24.0 us)
Async XLA Ops:
  7.2 3.7 copy-start.35
  7.2 3.8 copy-start.36
  7.2 3.8 copy-start.37
  7.2 15.5 %copy-start.33 = (bf16[3,512]{1,0:T(4,128)(2,1)S(1)}, bf16[3,512]{1,0:T(4,128)(2,1)}, u32[]{:S(2)}) copy-start(bf16[3,512]{1,0:T(4,128)(2,1)} %param.20) | copy-start | bytes 9220
  7.2 15.5 %copy-start.40 = (s32[1,3]{1,0:T(1,128)S(1)}, s32[1,3]{1,0:T(1,128)}, u32[]{:S(2)}) copy-start(s32[1,3]{1,0:T(1,128)} %param.15) | copy-start | bytes 40
  7.2 15.8 %copy-start = (bf16[1,512,2048]{2,1,0:T(8,128)(2,1)S(1)}, bf16[1,512,2048]{2,1,0:T(8,128)(2,1)}, u32[]{:S(2)}) copy-start(bf16[1,512,2048]{2,1,0:T(8,128)(2,1)} %param.14) | copy-start | bytes 6291460
  7.2 52.1 %all-gather.21.cloned.1.call-start = ((), (), s32[]{:S(2)}) async-start(), calls=%async_computation.6 | async-start | bytes 7864320 | tf_op jit(solution)/shard_map/all_gather | solution.py:84
  10.0 73.5 %all-gather.25.cloned.1.call-start = ((), (), s32[]{:S(2)}) async-start(), calls=%async_computation.8 | async-start | bytes 2621440 | tf_op jit(solution)/shard_map/all_gather | solution.py:85
  10.8 96.1 %all-gather.23.cloned.1.call-start = ((), (), s32[]{:S(2)}) async-start(), calls=%async_computation.7 | async-start | bytes 1572864 | tf_op jit(solution)/shard_map/all_gather | solution.py:132
  11.0 12.1 copy-start.29
  17.2 48.0 %copy-start.31 = (f32[4,1,512]{2,1,0:T(1,128)}, f32[4,1,512]{2,1,0:T(1,128)S(1)}, u32[]{:S(2)}) copy-start(f32[4,1,512]{2,1,0:T(1,128)S(1)} %convert_element_type.155) | copy-start | bytes 24580
  23.0 45.6 %copy-start.30 = (s32[512]{0:T(512)}, s32[512]{0:T(512)S(1)}, u32[]{:S(2)}) copy-start(s32[512]{0:T(512)S(1)} %get-tuple-element.65) | copy-start | bytes 6148
  24.1 41.1 %copy-start.26 = (f32[512]{0:T(512)}, f32[512]{0:T(512)S(1)}, u32[]{:S(2)}) copy-start(f32[512]{0:T(512)S(1)} %add_rsqrt_fusion) | copy-start | bytes 6148
  24.5 41.1 %copy-start.24 = (f32[512,32]{0,1:T(8,128)}, f32[512,32]{0,1:T(8,128)S(1)}, u32[]{:S(2)}) copy-start(f32[512,32]{0,1:T(8,128)S(1)} %get-tuple-element.89) | copy-start | bytes 196612
  24.5 41.1 %copy-start.25 = (f32[512,32]{0,1:T(8,128)}, f32[512,32]{0,1:T(8,128)S(1)}, u32[]{:S(2)}) copy-start(f32[512,32]{0,1:T(8,128)S(1)} %get-tuple-element.90) | copy-start | bytes 196612
  65.3 1.7 copy-start.12
  67.8 62.4 %all-gather.39.cloned.1.call-start = ((), (), s32[]{:S(2)}) async-start(), calls=%async_computation.22 | async-start | bytes 1572864 | tf_op jit(solution)/shard_map/all_gather | solution.py:133
  68.0 19.8 %copy-start.28 = (s32[1024]{0:T(1024)}, s32[1024]{0:T(1024)S(1)}, u32[]{:S(2)}) copy-start(s32[1024]{0:T(1024)S(1)} %fusion.77) | copy-start | bytes 12292
  90.0 74.9 %reduce-scatter.9.cloned.1.call-start = ((), (), s32[]{:S(2)}) async-start(), calls=%async_computation.12 | async-start | bytes 3145728 | tf_op jit(solution)/shard_map/reduce_scatter | solution.py:215
  106.9 2.4 copy-start.41
  108.8 2.7 copy-start.1
  108.8 2.7 copy-start.13
  111.0 1.8 copy-start.3
  114.3 85.2 %reduce-scatter.7.cloned.1.call-start = ((), (), s32[]{:S(2)}) async-start(), calls=%async_computation.11 | async-start | bytes 3145728 | tf_op jit(solution)/shard_map/reduce_scatter | solution.py:214
  130.2 2.5 copy-start.4
  132.7 1.9 copy-start.2
  132.8 2.2 copy-start.22
  133.3 2.9 copy-start.10
  136.1 1.0 copy-start.11
  138.6 1.6 copy-start.23
  138.6 120.8 %all-gather.27.cloned.1.call-start = ((), (), s32[]{:S(2)}) async-start(), calls=%async_computation.9 | async-start | bytes 10485760 | tf_op jit(solution)/shard_map/all_gather | solution.py:86
  139.3 179.9 %all-gather.29.cloned.1.call-start = ((), (), s32[]{:S(2)}) async-start(), calls=%async_computation.10 | async-start | bytes 10485760 | tf_op jit(solution)/shard_map/all_gather | solution.py:87
  140.1 234.2 %reduce-scatter.13.cloned.1.call-start = ((), (), s32[]{:S(2)}) async-start(), calls=%async_computation.16 | async-start | bytes 4718592 | tf_op jit(solution)/shard_map/reduce_scatter | solution.py:241
  140.1 2.4 copy-start.5
  142.6 1.6 copy-start.7
  147.4 322.2 %reduce-scatter.11.cloned.1.call-start = ((), (), s32[]{:S(2)}) async-start(), calls=%async_computation.14 | async-start | bytes 14155776 | tf_op jit(solution)/shard_map/reduce_scatter | solution.py:240
  149.4 2.0 copy-start.19
  151.5 0.8 copy-start.20
  216.0 0.7 copy-start.34
  216.0 43.3 %copy-start.27 = (f32[512]{0:T(512)S(1)}, f32[512]{0:T(512)}, u32[]{:S(2)}) copy-start(f32[512]{0:T(512)} %copy-done.26) | copy-start | bytes 6148
  216.0 43.3 %copy-start.32 = (f32[4,1,512]{2,1,0:T(1,128)S(1)}, f32[4,1,512]{2,1,0:T(1,128)}, u32[]{:S(2)}) copy-start(f32[4,1,512]{2,1,0:T(1,128)} %copy-done.31) | copy-start | bytes 24580
  216.1 373.4 %reduce-scatter.15.cloned.1.call-start = ((), (), s32[]{:S(2)}) async-start(), calls=%async_computation.18 | async-start | bytes 18874368 | tf_op jit(solution)/shard_map/reduce_scatter | solution.py:242
  328.6 1.3 copy-start.43
  338.7 370.1 %reduce-scatter.17.cloned.1.call-start = ((), (), s32[]{:S(2)}) async-start(), calls=%async_computation.20 | async-start | bytes 18874368 | tf_op jit(solution)/shard_map/reduce_scatter | solution.py:243
  351.8 380.0 %all-gather.33.cloned.1.call-start = ((), (), s32[]{:S(2)}) async-start(), calls=%async_computation.17 | async-start | bytes 1572864 | tf_op jit(solution)/shard_map/all_gather | solution.py:250
  374.3 515.3 %all-reduce.6.cloned.1.call-start = ((), (), s32[]{:S(2)}) async-start(), calls=%async_computation.13 | async-start | bytes 8388608 | tf_op jit(solution)/shard_map/psum | solution.py:229
  374.3 7.8 copy-start.14
  374.3 7.8 copy-start.16
  374.3 7.8 copy-start.18
  391.0 548.1 %all-gather.31.cloned.1.call-start = ((), (), s32[]{:S(2)}) async-start(), calls=%async_computation.15 | async-start | bytes 4718592 | tf_op jit(solution)/shard_map/all_gather | solution.py:249
  469.7 756.3 %all-gather.41.cloned.1.call-start = ((), (), s32[]{:S(2)}) async-start(), calls=%async_computation.23 | async-start | bytes 20971520 | tf_op jit(solution)/shard_map/all_gather | solution.py:172
  469.8 7.8 copy-start.21
  481.0 227.9 %copy-start.38 = (bf16[512]{0:T(512)(128)(2,1)S(1)}, bf16[512]{0:T(512)(128)(2,1)}, u32[]{:S(2)}) copy-start(bf16[512]{0:T(512)(128)(2,1)} %param.22) | copy-start | bytes 3076
  481.0 228.0 %copy-start.39 = (bf16[512]{0:T(512)(128)(2,1)S(1)}, bf16[512]{0:T(512)(128)(2,1)}, u32[]{:S(2)}) copy-start(bf16[512]{0:T(512)(128)(2,1)} %param.26) | copy-start | bytes 3076
  481.0 228.0 %copy-start.42 = (u32[32]{0:T(128)S(1)}, u32[32]{0:T(128)}, u32[]{:S(2)}) copy-start(u32[32]{0:T(128)} %constant.160) | copy-start | bytes 388
  481.0 239.8 %copy-start.15 = (bf16[512,1,512]{2,0,1:T(8,128)(2,1)S(1)}, bf16[512,1,512]{2,0,1:T(8,128)(2,1)}, u32[]{:S(2)}) copy-start(bf16[512,1,512]{2,0,1:T(8,128)(2,1)} %copy.63) | copy-start | bytes 1572868
  481.0 239.8 %copy-start.17 = (bf16[512,1,512]{2,0,1:T(8,128)(2,1)S(1)}, bf16[512,1,512]{2,0,1:T(8,128)(2,1)}, u32[]{:S(2)}) copy-start(bf16[512,1,512]{2,0,1:T(8,128)(2,1)} %copy.61) | copy-start | bytes 1572868
  481.0 801.3 %all-gather.35.cloned.1.call-start = ((), (), s32[]{:S(2)}) async-start(), calls=%async_computation.19 | async-start | bytes 6291456 | tf_op jit(solution)/shard_map/all_gather | solution.py:251
  589.5 751.0 %all-gather.37.cloned.1.call-start = ((), (), s32[]{:S(2)}) async-start(), calls=%async_computation.21 | async-start | bytes 6291456 | tf_op jit(solution)/shard_map/all_gather | solution.py:252
  889.5 3.8 copy-start.6
  889.5 4.1 copy-start.8
  1345.8 6.2 copy-start.9
Sparse Core Ops, SparseCore 0:
  10.2 49.1 all-gather.20
  60.9 22.5 all-gather.24
  85.6 21.2 all-gather.22
  108.9 21.2 all-gather.38
  132.9 31.9 reduce-scatter.8
  167.5 31.8 reduce-scatter.6
  201.0 58.2 all-gather.26
  260.9 58.2 all-gather.28
  323.1 51.0 reduce-scatter.12
  377.6 92.0 reduce-scatter.10
  473.2 116.1 reduce-scatter.14
  592.9 115.9 reduce-scatter.16
  710.4 21.2 all-gather.32
  734.5 154.9 all-reduce.5
  890.9 46.3 all-gather.30
  939.3 286.5 all-gather.40
  1227.4 54.8 all-gather.34
  1283.7 56.7 all-gather.36
